TPU v7x, 32 devices: a whole 2x2x4 slice. The times are simulated.
32 devices in a mesh: seq: 8 (over z, y), span: 4 (over x, core).
Axes of the slice: x: 2, y: 2, z: 4, core: 2. Of those that a mesh axis runs over, the one named last changes fastest.
Arguments:
- inputs: bfloat16 [8, 512, 768], P('seq', 'span'), may hold values from -6 to 6
- norm_gain: float32 [768], replicated, may hold values from 0.1 to 1.9
- z_weight: bfloat16 [768, 1536], P(('seq', 'span')), may hold values from -0.21875 to 0.21875
- xbc_weight: bfloat16 [768, 1792], P(('seq', 'span')), may hold values from -0.21875 to 0.21875
- dt_weight: bfloat16 [768, 24], P(('seq', 'span')), may hold values from -0.21875 to 0.21875
- conv_weight: float32 [4, 1792], replicated, may hold values from -3 to 3
- conv_bias: float32 [1792], replicated, may hold values from -3 to 3
- dt_bias: float32 [24], replicated, may hold values from -6 to -1
- a_log: float32 [24], replicated, may hold values from -1 to 1.5
- skip_gain: float32 [24], replicated, may hold values from 0.5 to 1.5
- gate_gain: float32 [1536], replicated, may hold values from 0.1 to 1.9
- out_weight: bfloat16 [1536, 768], P(('seq', 'span')), may hold values from -0.15625 to 0.15625
- segments: int32 [8, 512], P('seq', 'span'), may hold values from 0 to 3, never falling along the last dimension, each value on 1 to 256 neighbouring positions
- cotangent: bfloat16 [8, 512, 768], P('seq', 'span'), may hold values from -6 to 6
Outputs:
- output: bfloat16 [8, 512, 768], P('seq', 'span')
- input_grad: float32 [8, 512, 768], P('seq', 'span')
- norm_gain_grad: float32 [768], replicated
- z_weight_grad: float32 [768, 1536], P(('seq', 'span'))
- xbc_weight_grad: float32 [768, 1792], P(('seq', 'span'))
- dt_weight_grad: float32 [768, 24], P(('seq', 'span'))
- conv_weight_grad: float32 [4, 1792], replicated
- conv_bias_grad: float32 [1792], replicated
- dt_bias_grad: float32 [24], replicated
- a_log_grad: float32 [24], replicated
- skip_gain_grad: float32 [24], replicated
- gate_gain_grad: float32 [1536], replicated
- out_weight_grad: float32 [1536, 768], P(('seq', 'span'))
Inputs may be any that keep to these rules, and one draw needn't show every extreme that they name: `segments`: within a sequence the numbers never fall; a document is one run of equal numbers, of 1 to 256 tokens.
All inputs are finite; a program needn't handle non-finite values.
Results may differ from a plain program's by a relative error of at most 0.0094.
Values may be sent and summed in bfloat16 or wider, within the bound.
A program may use at most 128 MiB of HBM per device.

v0:
```python
import jax
import jax.numpy as jnp
from jax import lax
from jax.sharding import PartitionSpec as P

DI = 1536
H = 24
P_SIZE = 64
N = 128
KW = 4
CH = 1792
EPSILON = 1e-05
HIGHEST = lax.Precision.HIGHEST
CONTRACT_LAST = (((1,), (1,)), ((), ()))
CONTRACT_FIRST = (((0,), (0,)), ((), ()))


def shifted(x, axis, by):
    devices = lax.axis_size(axis)
    pairs = [(i, i + by) for i in range(devices) if 0 <= i + by < devices]
    return lax.ppermute(x, axis, pairs)


def carried_in(part, axis, combine, identity, reverse):
    count = lax.axis_size(axis)
    place = lax.axis_index(axis)
    ahead = count - 1 - place if reverse else place
    gathered = jax.tree.map(lambda a: lax.all_gather(a, axis), part)
    state = jax.tree.map(lambda a, e: jnp.zeros_like(a) + jnp.asarray(e, a.dtype), part, identity)

    def one(turn, state):
        source = count - 1 - turn if reverse else turn
        return combine(
            state, jax.tree.map(lambda a: lax.dynamic_index_in_dim(a, source, 0, False), gathered)
        )

    return lax.fori_loop(0, ahead, one, state)


def input_norm(values, gain):
    scale = lax.rsqrt(jnp.mean(values * values, axis=-1, keepdims=True) + EPSILON)
    return values * scale * gain


def gated_norm(mixed, gate, gain):
    gated = mixed * jax.nn.silu(gate)
    scale = lax.rsqrt(jnp.mean(gated * gated, axis=-1, keepdims=True) + EPSILON)
    return gated * scale * gain


def conv_and_step(conv_in, edge, seg_now, seg_edge, conv_weight, conv_bias, dt_raw, dt_bias, a_log):
    taps = conv_weight.shape[0]
    length = conv_in.shape[0]
    padded = jnp.concatenate([edge, conv_in], axis=0)
    seg_all = jnp.concatenate([seg_edge, seg_now], axis=0)
    total = jnp.zeros_like(conv_in) + conv_bias
    for offset in range(taps):
        same = (seg_all[offset : offset + length] == seg_now).astype(jnp.float32)
        total = total + conv_weight[offset] * padded[offset : offset + length] * same[:, None]
    activated = jax.nn.silu(total)
    step_size = jax.nn.softplus(dt_raw + dt_bias)
    log_decay = -jnp.exp(a_log) * step_size
    return (activated, step_size, log_decay)


def scan_local(activated, step_size, log_decay, seg_now, seg_before, skip_gain):
    length = activated.shape[0]
    inner = activated[:, :DI].reshape(length, H, P_SIZE)
    in_state = activated[:, DI : DI + N]
    out_state = activated[:, DI + N :]
    cumul = jnp.cumsum(log_decay, axis=0)
    cum_heads = cumul.T
    later = lax.broadcasted_iota(jnp.int32, (length, length), 0)
    earlier = lax.broadcasted_iota(jnp.int32, (length, length), 1)
    allowed = (later >= earlier) & (seg_now[:, None] == seg_now[None, :])
    mask_three = allowed[None, :, :]
    spread = cum_heads[:, :, None] - cum_heads[:, None, :]
    decay = jnp.where(mask_three, jnp.exp(jnp.where(mask_three, spread, 0.0)), 0.0)
    intersection = jnp.dot(
        out_state, in_state.T, precision=HIGHEST, preferred_element_type=jnp.float32
    )
    mixing = intersection[None, :, :] * decay * step_size.T[:, None, :]
    result = jnp.einsum("hts,shp->thp", mixing, inner, precision=HIGHEST)
    result = result + skip_gain[None, :, None] * inner
    carried = jnp.exp(cumul) * (seg_now == seg_before).astype(jnp.float32)[:, None]
    tail = (
        jnp.exp(cumul[-1][None, :] - cumul)
        * (seg_now == seg_now[-1]).astype(jnp.float32)[:, None]
        * step_size
    )
    local_end = jnp.einsum("sh,shp,sn->hpn", tail, inner, in_state, precision=HIGHEST)
    return (result, local_end, carried)


def add_carry(result, carried, out_state, state_in):
    return result + carried[:, :, None] * jnp.einsum(
        "tn,hpn->thp", out_state, state_in, precision=HIGHEST
    )


def span_full(
    conv_in,
    edge,
    dt_raw,
    conv_weight,
    conv_bias,
    dt_bias,
    a_log,
    skip_gain,
    state_in,
    seg_now,
    seg_edge,
):
    activated, step_size, log_decay = conv_and_step(
        conv_in, edge, seg_now, seg_edge, conv_weight, conv_bias, dt_raw, dt_bias, a_log
    )
    result, local_end, carried = scan_local(
        activated, step_size, log_decay, seg_now, seg_edge[-1], skip_gain
    )
    mixed = add_carry(result, carried, activated[:, DI + N :], state_in)
    state_end = carried[-1][:, None, None] * state_in + local_end
    return (mixed.reshape(mixed.shape[0], DI), state_end)


def chain_states(earlier, later):
    return (earlier[0] * later[0], later[0][:, :, None, None] * earlier[1] + later[1])


def body(
    inputs,
    norm_gain,
    z_weight,
    xbc_weight,
    dt_weight,
    conv_weight,
    conv_bias,
    dt_bias,
    a_log,
    skip_gain,
    gate_gain,
    out_weight,
    segments,
    cotangent,
):
    seqs_here, span_len, width = inputs.shape
    rows = seqs_here * span_len
    flat = inputs.astype(jnp.float32).reshape(rows, width)
    normed = input_norm(flat, norm_gain).astype(jnp.bfloat16)
    pieces = (
        lax.all_gather(z_weight, ("seq", "span"), axis=0, tiled=True),
        lax.all_gather(xbc_weight, ("seq", "span"), axis=0, tiled=True),
        lax.all_gather(dt_weight, ("seq", "span"), axis=0, tiled=True),
    )
    columns = normed
    gate, conv_wide, dt_raw = tuple(
        (jnp.dot(columns, piece, preferred_element_type=jnp.float32) for piece in pieces)
    )
    conv_in = conv_wide.astype(jnp.bfloat16).reshape(seqs_here, span_len, CH)
    seg_wire = (segments[:, span_len - KW + 1 :] + 1).astype(jnp.bfloat16)
    edge, seg_edge = shifted((conv_in[:, span_len - KW + 1 :], seg_wire), "span", 1)
    conv_float = conv_in.astype(jnp.float32)
    edge_float = edge.astype(jnp.float32)
    seg_edge_float = seg_edge.astype(jnp.float32)
    seg_now = (segments + 1).astype(jnp.float32)
    dt_spans = dt_raw.reshape(seqs_here, span_len, H)
    prepare = jax.vmap(conv_and_step, in_axes=(0, 0, 0, 0, None, None, 0, None, None))
    activated, step_size, log_decay = prepare(
        conv_float,
        edge_float,
        seg_now,
        seg_edge_float,
        conv_weight,
        conv_bias,
        dt_spans,
        dt_bias,
        a_log,
    )
    local_scan = jax.vmap(scan_local, in_axes=(0, 0, 0, 0, 0, None))
    result, local_end, carried = local_scan(
        activated, step_size, log_decay, seg_now, seg_edge_float[:, -1], skip_gain
    )
    decay_total = carried[:, -1]
    identity = (jnp.ones_like(decay_total), jnp.zeros_like(local_end))
    state_in = carried_in((decay_total, local_end), "span", chain_states, identity, False)[1]
    out_state = activated[:, :, DI + N :]
    mixed = jax.vmap(add_carry)(result, carried, out_state, state_in).reshape(rows, DI)
    mix_bf = gated_norm(mixed, gate, gate_gain).astype(jnp.bfloat16)
    columns = mix_bf
    projected = jnp.dot(
        columns,
        lax.all_gather(out_weight, ("seq", "span"), axis=0, tiled=True),
        preferred_element_type=jnp.float32,
    )
    output = (flat + projected).astype(jnp.bfloat16).reshape(inputs.shape)
    grad_out = cotangent.reshape(rows, width)
    grad_mix = lax.dot_general(
        grad_out,
        lax.all_gather(out_weight, ("seq", "span"), axis=0, tiled=True),
        CONTRACT_LAST,
        preferred_element_type=jnp.float32,
    )
    unused_norm, gate_pull = jax.vjp(gated_norm, mixed, gate, gate_gain)
    grad_mixed, grad_gate, gate_gain_grad = gate_pull(grad_mix)
    grad_heads = grad_mixed.reshape(seqs_here, span_len, H, P_SIZE)
    summary = jnp.einsum("sth,sthp,stn->shpn", carried, grad_heads, out_state, precision=HIGHEST)
    state_grad = carried_in((decay_total, summary), "span", chain_states, identity, True)[1]

    def local_span(conv_a, edge_a, dt_a, weight_a, bias_a, dtb_a, alog_a, skip_a, state_a):
        batched = jax.vmap(span_full, in_axes=(0, 0, 0, None, None, None, None, None, 0, 0, 0))
        return batched(
            conv_a,
            edge_a,
            dt_a,
            weight_a,
            bias_a,
            dtb_a,
            alog_a,
            skip_a,
            state_a,
            seg_now,
            seg_edge_float,
        )

    unused_span, span_pull = jax.vjp(
        local_span,
        conv_float,
        edge_float,
        dt_spans,
        conv_weight,
        conv_bias,
        dt_bias,
        a_log,
        skip_gain,
        state_in,
    )
    grads = span_pull((grad_mixed.reshape(seqs_here, span_len, DI), state_grad))
    edge_back = shifted(grads[1], "span", -1)
    conv_grad = grads[0].at[:, span_len - KW + 1 :].add(edge_back)
    gate_bf = grad_gate.astype(jnp.bfloat16)
    conv_bf = conv_grad.reshape(rows, CH).astype(jnp.bfloat16)
    dt_bf = grads[2].reshape(rows, H).astype(jnp.bfloat16)
    grad_joined = jnp.concatenate([gate_bf, conv_bf, dt_bf], axis=1)
    out_full = lax.dot_general(mix_bf, grad_out, CONTRACT_FIRST, preferred_element_type=jnp.float32)
    in_full = lax.dot_general(
        normed, grad_joined, CONTRACT_FIRST, preferred_element_type=jnp.float32
    )
    out_weight_grad, in_owned = (
        lax.psum_scatter(out_full, ("seq", "span"), scatter_dimension=0, tiled=True),
        lax.psum_scatter(in_full, ("seq", "span"), scatter_dimension=0, tiled=True),
    )
    z_weight_grad = in_owned[:, :DI]
    xbc_weight_grad = in_owned[:, DI : DI + CH]
    dt_weight_grad = in_owned[:, DI + CH :]
    pieces = lax.all_gather((z_weight, xbc_weight, dt_weight), ("seq", "span"), axis=0, tiled=True)
    partial_sum = lax.dot_general(
        gate_bf, pieces[0], CONTRACT_LAST, preferred_element_type=jnp.float32
    )
    partial_sum = partial_sum + lax.dot_general(
        conv_bf, pieces[1], CONTRACT_LAST, preferred_element_type=jnp.float32
    )
    normed_grad = partial_sum + lax.dot_general(
        dt_bf, pieces[2], CONTRACT_LAST, preferred_element_type=jnp.float32
    )
    unused_input, norm_pull = jax.vjp(input_norm, flat, norm_gain)
    grad_flat, norm_gain_part = norm_pull(normed_grad)
    input_grad = (grad_out.astype(jnp.float32) + grad_flat).reshape(inputs.shape)
    summed = lax.psum(
        (norm_gain_part, grads[3], grads[4], grads[5], grads[6], grads[7], gate_gain_grad),
        ("seq", "span"),
    )
    return (
        output,
        input_grad,
        summed[0],
        z_weight_grad,
        xbc_weight_grad,
        dt_weight_grad,
        summed[1],
        summed[2],
        summed[3],
        summed[4],
        summed[5],
        summed[6],
        out_weight_grad,
    )


def solution(mesh):
    in_specs = (
        P("seq", "span", None),
        P(),
        P(("seq", "span"), None),
        P(("seq", "span"), None),
        P(("seq", "span"), None),
        P(),
        P(),
        P(),
        P(),
        P(),
        P(),
        P(("seq", "span"), None),
        P("seq", "span"),
        P("seq", "span", None),
    )
    out_specs = (
        P("seq", "span", None),
        P("seq", "span", None),
        P(),
        P(("seq", "span"), None),
        P(("seq", "span"), None),
        P(("seq", "span"), None),
        P(),
        P(),
        P(),
        P(),
        P(),
        P(),
        P(("seq", "span"), None),
    )
    return jax.shard_map(body, mesh=mesh, in_specs=in_specs, out_specs=out_specs, check_vma=False)
```

profile of v0, /device:TPU:0, one launch (start us, length us, event | category | flops | bytes accessed | tf_op | source)
XLA Modules:
  0.0 651.5 jit_solution(18130649369982136000)
XLA Ops:
  8.7 2.4 collective-permute-start.1
  12.3 43.7 %all_gather.33 = bf16[768,24]{1,0:T(8,128)(2,1)S(1)} all-gather(bf16[24,24]{1,0:T(8,128)(2,1)} %param.24), channel_id=1, replica_groups=mesh['seq'=8,'span'=4] {'seq','span'}, dimensions={0}, use_global_device_ids=true | all-gather | bytes 38016 | tf_op jit(solution)/shard_map/all_gather | solution.py:152
  61.2 2.0 fusion.120
  63.3 8.4 %all-gather.8.cloned.1.call-done = bf16[768,1792]{1,0:T(8,128)(2,1)} async-done(((bf16[24,1792]{1,0:T(8,128)(2,1)}), bf16[768,1792]{1,0:T(8,128)(2,1)}) %all-gather.8.cloned.1.call-update) | async-done | bytes 2752528 | tf_op jit(solution)/shard_map/all_gather | solution.py:151
  71.7 2.5 convolution_convert_fusion
  74.3 2.1 collective-permute-start
  77.4 1.8 fusion.32
  79.5 1.7 fusion.66
  84.2 6.5 %all_gather.34 = f32[4,1,24]{2,1,0:T(1,128)S(1)} all-gather(f32[1,1,24]{2,1,0:T(1,128)S(1)} %copy.113), channel_id=1, replica_groups=mesh['seq'=8,'span'=4] {'span'}, dimensions={0}, use_global_device_ids=true | all-gather | bytes 480 | tf_op jit(solution)/shard_map/all_gather | solution.py:28
  91.0 19.8 %all-gather.14.cloned.1.call-done = f32[96,64,128]{2,1,0:T(8,128)} async-done(((f32[24,64,128]{2,1,0:T(8,128)}), f32[96,64,128]{2,1,0:T(8,128)}) %all-gather.14.cloned.1.call-update) | async-done | bytes 3145744 | tf_op jit(solution)/shard_map/all_gather | solution.py:28
  111.8 3.3 fusion.19
  115.5 55.3 %all-gather.10.cloned.1.call-done = bf16[768,1536]{1,0:T(8,128)(2,1)} async-done(((bf16[24,1536]{1,0:T(8,128)(2,1)}), bf16[768,1536]{1,0:T(8,128)(2,1)}) %all-gather.10.cloned.1.call-update) | async-done | bytes 2359312 | tf_op jit(solution)/shard_map/all_gather | solution.py:150
  170.8 3.1 multiply_reduce_fusion.11
  174.4 54.9 %all-gather.12.cloned.1.call-done = bf16[1536,768]{1,0:T(8,128)(2,1)} async-done(((bf16[48,768]{1,0:T(8,128)(2,1)}), bf16[1536,768]{1,0:T(8,128)(2,1)}) %all-gather.12.cloned.1.call-update) | async-done | bytes 2359312 | tf_op jit(solution)/shard_map/all_gather | solution.py:191
  229.3 3.4 multiply_reduce_fusion.7
  232.8 2.2 fusion.44
  235.0 1.4 copy.119
  236.5 2.6 fusion.50
  240.3 2.3 copy.117
  242.6 2.4 mul.724
  245.0 2.4 copy.118
  247.5 4.3 fusion.40
  254.8 1.4 convolution_bitcast_fusion.2
  256.2 10.4 %all-gather.16.cloned.1.call-done = f32[96,64,128]{2,1,0:T(8,128)} async-done(((f32[24,64,128]{2,1,0:T(8,128)}), f32[96,64,128]{2,1,0:T(8,128)}) %all-gather.16.cloned.1.call-update) | async-done | bytes 3145744 | tf_op jit(solution)/shard_map/all_gather | solution.py:28
  266.7 6.2 while.28
  273.7 2.3 multiply_reduce_fusion.6
  276.0 1.4 fusion.24
  277.5 2.8 fusion.13
  280.3 2.4 copy.122
  282.9 2.8 fusion.135
  289.5 2.0 fusion.140
  292.9 1.5 bitcast_add_fusion.2
  294.4 1.4 copy.125
  295.8 2.6 reduce_window_sum.30
  298.4 1.5 copy.126
  301.2 1.9 slice_bitcast_fusion
  303.1 2.1 fusion.137
  305.2 1.4 copy.127
  306.6 1.5 fusion.103
  309.4 6.8 %fusion.33 = f32[768,3352]{1,0:T(8,128)} fusion(bf16[128,24]{1,0:T(8,128)(2,1)} %copy.127, bf16[128,1792]{1,0:T(8,128)(2,1)} %scatter-add.4, bf16[128,1536]{1,0:T(8,128)(2,1)} %get-tuple-element.263, bf16[1,128,768]{2,1,0:T(8,128)(2,1)} %param.20, f32[768]{0:T(1024)S(1)} %copy-done.31, f32[128]{0:T(128)S(1)} %copy-done.59), kind=kOutput, calls=%fused_computation.56 | convolution fusion | flops 661997568 | bytes 11355648 | tf_op jit(solution)/shard_map/dot_general | solution.py:244
  317.2 3.1 fusion.80
  320.3 1.5 reduce_sum.231
  323.2 2.0 fusion.23
  328.6 42.0 %all-reduce.15 = (f32[768]{0:T(1024)}, f32[4,1792]{1,0:T(4,128)}, f32[1792]{0:T(1024)}, f32[24]{0:T(128)}, f32[24]{0:T(128)}, /*index=5*/f32[24]{0:T(128)}, f32[1536]{0:T(1024)}) all-reduce(f32[768]{0:T(1024)S(1)} %get-tuple-element.219, f32[4,1792]{1,0:T(4,128)S(1)} %pad_add_fusion.2, ...), channel_id=1, replica_groups=mesh['seq'=8,'span'=4] {'seq','span'}, use_global_device_ids=true, to_apply=%region_18.19 | all-reduce | flops 11336 | bytes 90688 | tf_op jit(solution)/shard_map/psum | solution.py:267
  371.5 160.5 %all-reduce.18.cloned.1.call-done = f32[768,3352]{1,0:T(8,128)} async-done(((f32[768,3352]{1,0:T(8,128)}), f32[768,3352]{1,0:T(8,128)}) %all-reduce.18.cloned.1.call-update) | async-done | bytes 10297360
  533.4 1.7 dynamic-slice.10
  535.1 1.6 constant_dynamic-slice_fusion
  536.7 108.0 %reduce-scatter.2.cloned.1.call-done = f32[48,768]{1,0:T(8,128)} async-done(((f32[1536,768]{1,0:T(8,128)}), f32[48,768]{1,0:T(8,128)}) %reduce-scatter.2.cloned.1.call-update) | async-done | bytes 147472 | tf_op jit(solution)/shard_map/reduce_scatter | solution.py:248
  (271 shorter events, 40.6 us)
Async XLA Ops:
  7.2 64.6 %all-gather.8.cloned.1.call-start = ((), (), s32[]{:S(2)}) async-start(), calls=%async_computation.1 | async-start | bytes 2838528 | tf_op jit(solution)/shard_map/all_gather | solution.py:151
  7.9 102.9 %all-gather.14.cloned.1.call-start = ((), (), s32[]{:S(2)}) async-start(), calls=%async_computation.5 | async-start | bytes 3932160 | tf_op jit(solution)/shard_map/all_gather | solution.py:28
  8.7 51.8 %collective-permute-start.1 = (bf16[1,3]{1,0:T(2,128)(2,1)S(1)}, bf16[1,3]{1,0:T(2,128)(2,1)S(1)}, u32[]{:S(2)}, u32[]{:S(2)}) collective-permute-start(bf16[1,3]{1,0:T(2,128)(2,1)S(1)} %add_convert_fusion.1), channel_id=1, source_target_pairs={{0,1},{1,2},{2,3},{4,5},{5,6},{6,7},{8,9},{9,10},{10,11},{12,13},{... | collective-permute-start | bytes 26 | tf_op jit(solution)/shard_map/ppermute | solution.py:21
  57.1 17.1 %copy-start.86 = (f32[128]{0:T(128)}, f32[128]{0:T(128)S(1)}, u32[]{:S(2)}) copy-start(f32[128]{0:T(128)S(1)} %fusion.74) | copy-start | bytes 1540
  57.8 16.4 %copy-start.58 = (f32[128]{0:T(128)}, f32[128]{0:T(128)S(1)}, u32[]{:S(2)}) copy-start(f32[128]{0:T(128)S(1)} %fusion.123) | copy-start | bytes 1540
  59.0 15.2 %copy-start.27 = (f32[128,24]{0,1:T(8,128)}, f32[128,24]{0,1:T(8,128)S(1)}, u32[]{:S(2)}) copy-start(f32[128,24]{0,1:T(8,128)S(1)} %convolution_add_fusion.3) | copy-start | bytes 36868
  60.5 16.8 %copy-start.39 = (f32[1792]{0:T(1024)}, f32[1792]{0:T(1024)S(1)}, u32[]{:S(2)}) copy-start(f32[1792]{0:T(1024)S(1)} %get-tuple-element.221) | copy-start | bytes 21508
  60.5 16.8 %copy-start.41 = (f32[1792]{0:T(1024)}, f32[1792]{0:T(1024)S(1)}, u32[]{:S(2)}) copy-start(f32[1792]{0:T(1024)S(1)} %get-tuple-element.222) | copy-start | bytes 21508
  60.5 16.8 %copy-start.43 = (f32[1792]{0:T(1024)}, f32[1792]{0:T(1024)S(1)}, u32[]{:S(2)}) copy-start(f32[1792]{0:T(1024)S(1)} %get-tuple-element.223) | copy-start | bytes 21508
  60.5 16.8 %copy-start.45 = (f32[1792]{0:T(1024)}, f32[1792]{0:T(1024)S(1)}, u32[]{:S(2)}) copy-start(f32[1792]{0:T(1024)S(1)} %get-tuple-element.224) | copy-start | bytes 21508
  60.5 13.7 %copy-start.80 = (f32[24]{0:T(128)}, f32[24]{0:T(128)S(1)}, u32[]{:S(2)}) copy-start(f32[24]{0:T(128)S(1)} %slice_bitcast_fusion.1) | copy-start | bytes 292
  61.2 16.1 %copy-start.66 = (f32[128]{0:T(128)}, f32[128]{0:T(128)S(1)}, u32[]{:S(2)}) copy-start(f32[128]{0:T(128)S(1)} %get-tuple-element.271) | copy-start | bytes 1540
  61.2 16.1 %copy-start.69 = (f32[128]{0:T(128)}, f32[128]{0:T(128)S(1)}, u32[]{:S(2)}) copy-start(f32[128]{0:T(128)S(1)} %get-tuple-element.272) | copy-start | bytes 1540
  61.2 16.1 %copy-start.72 = (f32[128]{0:T(128)}, f32[128]{0:T(128)S(1)}, u32[]{:S(2)}) copy-start(f32[128]{0:T(128)S(1)} %get-tuple-element.273) | copy-start | bytes 1540
  63.2 11.1 %copy-start.65 = (f32[128]{0:T(128)}, f32[128]{0:T(128)S(1)}, u32[]{:S(2)}) copy-start(f32[128]{0:T(128)S(1)} %get-tuple-element.276) | copy-start | bytes 1540
  63.2 14.2 %copy-start.75 = (f32[128]{0:T(128)}, f32[128]{0:T(128)S(1)}, u32[]{:S(2)}) copy-start(f32[128]{0:T(128)S(1)} %get-tuple-element.277) | copy-start | bytes 1540
  63.2 19.6 %copy-start.81 = (f32[128]{0:T(128)}, f32[128]{0:T(128)S(1)}, u32[]{:S(2)}) copy-start(f32[128]{0:T(128)S(1)} %get-tuple-element.278) | copy-start | bytes 1540
  63.3 16.3 %copy-start.34 = (f32[128,24]{0,1:T(8,128)}, f32[128,24]{0,1:T(8,128)S(1)}, u32[]{:S(2)}) copy-start(f32[128,24]{0,1:T(8,128)S(1)} %get-tuple-element.269) | copy-start | bytes 36868
  63.3 48.5 %copy-start.36 = (f32[128,24]{0,1:T(8,128)}, f32[128,24]{0,1:T(8,128)S(1)}, u32[]{:S(2)}) copy-start(f32[128,24]{0,1:T(8,128)S(1)} %get-tuple-element.268) | copy-start | bytes 36868
  63.3 48.5 %copy-start.62 = (f32[24,128]{1,0:T(8,128)}, f32[24,128]{1,0:T(8,128)S(1)}, u32[]{:S(2)}) copy-start(f32[24,128]{1,0:T(8,128)S(1)} %get-tuple-element.270) | copy-start | bytes 36868
  63.3 14.1 %copy-start.64 = (f32[1792]{0:T(1024)S(1)}, f32[1792]{0:T(1024)}, u32[]{:S(2)}) copy-start(f32[1792]{0:T(1024)} %param.26) | copy-start | bytes 21508
  74.3 4.9 copy-start.7
  74.3 3.0 collective-permute-start
  79.2 31.8 %copy-start.2 = (f32[1,128,1792]{2,1,0:T(8,128)}, f32[1,128,1792]{2,1,0:T(8,128)S(1)}, u32[]{:S(2)}) copy-start(f32[1,128,1792]{2,1,0:T(8,128)S(1)} %get-tuple-element.261) | copy-start | bytes 2752516
  81.2 89.5 %all-gather.10.cloned.1.call-start = ((), (), s32[]{:S(2)}) async-start(), calls=%async_computation.2 | async-start | bytes 2433024 | tf_op jit(solution)/shard_map/all_gather | solution.py:150
  82.0 147.3 %all-gather.12.cloned.1.call-start = ((), (), s32[]{:S(2)}) async-start(), calls=%async_computation.3 | async-start | bytes 2433024 | tf_op jit(solution)/shard_map/all_gather | solution.py:191
  82.6 184.0 %all-gather.16.cloned.1.call-start = ((), (), s32[]{:S(2)}) async-start(), calls=%async_computation.6 | async-start | bytes 3932160 | tf_op jit(solution)/shard_map/all_gather | solution.py:28
  82.7 29.1 %copy-start.60 = (f32[24,128]{1,0:T(8,128)}, f32[24,128]{1,0:T(8,128)S(1)}, u32[]{:S(2)}) copy-start(f32[24,128]{1,0:T(8,128)S(1)} %copy.108) | copy-start | bytes 36868
  82.8 29.0 %copy-start.56 = (pred[128,128]{1,0:T(8,128)(4,1)}, pred[128,128]{1,0:T(8,128)(4,1)S(1)}, u32[]{:S(2)}) copy-start(pred[128,128]{1,0:T(8,128)(4,1)S(1)} %fusion.94) | copy-start | bytes 49156
  91.0 20.8 %copy-start.47 = (f32[128,128]{1,0:T(8,128)}, f32[128,128]{1,0:T(8,128)S(1)}, u32[]{:S(2)}) copy-start(f32[128,128]{1,0:T(8,128)S(1)} %fusion.90) | copy-start | bytes 196612
  115.1 55.6 %copy-start.11 = (bf16[1,128,768]{2,1,0:T(8,128)(2,1)S(1)}, bf16[1,128,768]{2,1,0:T(8,128)(2,1)}, u32[]{:S(2)}) copy-start(bf16[1,128,768]{2,1,0:T(8,128)(2,1)} %param.20) | copy-start | bytes 589828
  115.2 55.6 %copy-start.31 = (f32[768]{0:T(1024)S(1)}, f32[768]{0:T(1024)}, u32[]{:S(2)}) copy-start(f32[768]{0:T(1024)} %param.21) | copy-start | bytes 9220
  115.4 58.4 %copy-start.19 = (f32[128,1536]{1,0:T(8,128)}, f32[128,1536]{1,0:T(8,128)S(1)}, u32[]{:S(2)}) copy-start(f32[128,1536]{1,0:T(8,128)S(1)} %copy.115) | copy-start | bytes 2359300
  115.5 113.8 %copy-start.22 = (bf16[1,128,768]{2,1,0:T(8,128)(2,1)S(1)}, bf16[1,128,768]{2,1,0:T(8,128)(2,1)}, u32[]{:S(2)}) copy-start(bf16[1,128,768]{2,1,0:T(8,128)(2,1)} %param.33) | copy-start | bytes 589828
  174.4 58.4 %copy-start.78 = (f32[128]{0:T(128)}, f32[128]{0:T(128)S(1)}, u32[]{:S(2)}) copy-start(f32[128]{0:T(128)S(1)} %fusion.124) | copy-start | bytes 1540
  236.4 17.6 %copy-start.9 = (f32[128,1536]{0,1:T(8,128)}, f32[128,1536]{0,1:T(8,128)S(1)}, u32[]{:S(2)}) copy-start(f32[128,1536]{0,1:T(8,128)S(1)} %copy.119) | copy-start | bytes 2359300
  239.1 292.9 %all-reduce.18.cloned.1.call-start = ((), (), s32[]{:S(2)}) async-start(), calls=%async_computation.7 | async-start | bytes 21233664
  242.6 4.9 copy-start.48
  242.6 4.9 copy-start.57
  242.6 4.9 copy-start.61
  242.6 4.9 copy-start.63
  247.5 6.6 %copy-start.17 = (f32[128,24,64]{0,2,1:T(8,128)S(1)}, f32[128,24,64]{0,2,1:T(8,128)}, u32[]{:S(2)}) copy-start(f32[128,24,64]{0,2,1:T(8,128)} %copy-done.16) | copy-start | bytes 2359300
  273.7 3.8 copy-start.10
  273.7 3.8 copy-start.89
  277.4 5.3 copy-start.14
  299.9 6.7 %collective-permute-start.2 = (f32[1,3,1792]{2,1,0:T(4,128)}, f32[1,3,1792]{2,1,0:T(4,128)}, u32[]{:S(2)}, u32[]{:S(2)}) collective-permute-start(f32[1,3,1792]{2,1,0:T(4,128)} %pad_add_fusion.1), channel_id=1, source_target_pairs={{1,0},{2,1},{3,2},{5,4},{6,5},{7,6},{9,8},{10,9},{11,10},{13,12},{... | collective-permute-start | bytes 64520 | tf_op jit(solution)/shard_map/ppermute | solution.py:21
  316.3 328.4 %reduce-scatter.2.cloned.1.call-start = ((), (), s32[]{:S(2)}) async-start(), calls=%async_computation.4 | async-start | bytes 4866048 | tf_op jit(solution)/shard_map/reduce_scatter | solution.py:248
  327.1 43.5 %copy-start.87 = (f32[128]{0:T(128)S(1)}, f32[128]{0:T(128)}, u32[]{:S(2)}) copy-start(f32[128]{0:T(128)} %copy-done.86) | copy-start | bytes 1540
  (55 other events, 124.7 us)
Sparse Core Ops, SparseCore 0:
  10.9 60.8 all-gather.7
  81.4 29.4 all-gather.13
  113.7 56.9 all-gather.9
  173.5 55.7 all-gather.11
  239.2 27.2 all-gather.15
  316.4 215.5 all-reduce.17
  538.1 106.5 reduce-scatter.1
where the time goes:
time: 653 us; the launch traced here: 652 us
  waiting for transfers between devices  420 us (64%)
  blocking collectives  92.2 us (14%)
  matrix products  47.6 us (7%)
  other arithmetic  35.4 us (5%)
  local copies, waits for them, and re-layouts  34.1 us (5%)
  between operations  15.4 us (2%)
  starting transfers between devices  6.53 us (1%)
    unnamed x8, waiting for transfers between devices  162 us
    reduce_scatter x1, waiting for transfers between devices, body(): lax.psum_scatter(out_full, ('seq', 'span'), scatter_dimension=0, tiled=True)  108 us
    all_gather x1, waiting for transfers between devices, body(): lax.all_gather(z_weight, ('seq', 'span'), axis=0, tiled=True)  55.3 us
    all_gather x1, waiting for transfers between devices, body(): lax.all_gather(out_weight, ('seq', 'span'), axis=0, tiled=True)  54.9 us
    all_gather x1, blocking collectives, body(): lax.all_gather(dt_weight, ('seq', 'span'), axis=0, tiled=True)  43.7 us
    psum x1, blocking collectives, body(): lax.psum((norm_gain_part, grads[3], grads[4], grads[5], grads[6], grads[7...  42 us
    all_gather x2, waiting for transfers between devices, carried_in(): gathered = jax.tree.map(lambda a: lax.all_gather(a, axis), part)  30.2 us
  transfers between devices with their start and end apart: 10, of which 8 were waited for; matrix products, arithmetic and copies ran while one was open for 9% of the time, Pallas kernels for 0%

commit v1 on v0

--- a/solution.py
+++ b/solution.py
@@ -13,6 +13,28 @@
 HIGHEST = lax.Precision.HIGHEST
 CONTRACT_LAST = (((1,), (1,)), ((), ()))
 CONTRACT_FIRST = (((0,), (0,)), ((), ()))
+
+
+def joined_along(tiles, dim):
+    tiles = jnp.moveaxis(tiles, 0, dim)
+    shape = tiles.shape
+    return tiles.reshape(*shape[:dim], shape[dim] * shape[dim + 1], *shape[dim + 2 :])
+
+
+def collected_by_bits(x, axis):
+    count = lax.axis_size(axis)
+    parts = x[None]
+    for level in range(count.bit_length() - 1):
+        bit = 1 << level
+        other = lax.ppermute(parts, axis, [(i, i ^ bit) for i in range(count)])
+        both = jnp.stack([parts, other])
+        upper = lax.axis_index(axis) >> level & 1
+        parts = jnp.where(upper == 0, both, both[::-1]).reshape(-1, *x.shape)
+    return parts
+
+
+def collect(value, axis, dim):
+    return joined_along(collected_by_bits(value, axis), dim)
 
 
 def shifted(x, axis, by):
@@ -187,9 +209,7 @@
     mix_bf = gated_norm(mixed, gate, gate_gain).astype(jnp.bfloat16)
     columns = mix_bf
     projected = jnp.dot(
-        columns,
-        lax.all_gather(out_weight, ("seq", "span"), axis=0, tiled=True),
-        preferred_element_type=jnp.float32,
+        columns, collect(out_weight, ("seq", "span"), 0), preferred_element_type=jnp.float32
     )
     output = (flat + projected).astype(jnp.bfloat16).reshape(inputs.shape)
     grad_out = cotangent.reshape(rows, width)

time: 653 us -> 707 us (1.083)
  waiting for transfers between devices: 420 us -> 465 us
  starting transfers between devices: 6.53 us -> 14.2 us
    ppermute x0 -> x5, waiting for transfers between devices: none -> 111 us  [collected_by_bits(): other = lax.ppermute(parts, axis, [(i, i ^ bit) for i in range(count)])]
    unnamed x8, waiting for transfers between devices: 162 us -> 97.5 us
    ppermute x0 -> x5, starting transfers between devices: none -> 7.62 us  [collected_by_bits(): other = lax.ppermute(parts, axis, [(i, i ^ bit) for i in range(count)])]
  transfers between devices with their start and end apart: 10 -> 15, of which waited for: 8 -> 13; matrix products, arithmetic and copies ran while one was open for 9% -> 8% of each run, Pallas kernels for 0% -> 0%
where the time goes in v1:
time: 707 us; the launch traced here: 705 us
  waiting for transfers between devices  465 us (66%)
  blocking collectives  90.1 us (13%)
  matrix products  46.7 us (7%)
  other arithmetic  36.7 us (5%)
  local copies, waits for them, and re-layouts  36.3 us (5%)
  between operations  15.4 us (2%)
  starting transfers between devices  14.2 us (2%)
    ppermute x5, waiting for transfers between devices, collected_by_bits(): other = lax.ppermute(parts, axis, [(i, i ^ bit) for i in range(count)])  111 us
    reduce_scatter x1, waiting for transfers between devices, body(): lax.psum_scatter(out_full, ('seq', 'span'), scatter_dimension=0, tiled=True)  108 us
    unnamed x8, waiting for transfers between devices  97.5 us
    all_gather x1, waiting for transfers between devices, body(): lax.all_gather(out_weight, ('seq', 'span'), axis=0, tiled=True)  55.2 us
    all_gather x1, waiting for transfers between devices, body(): lax.all_gather(z_weight, ('seq', 'span'), axis=0, tiled=True)  54.4 us
    all_gather x1, blocking collectives, body(): lax.all_gather(dt_weight, ('seq', 'span'), axis=0, tiled=True)  43.7 us
    psum x1, blocking collectives, body(): lax.psum((norm_gain_part, grads[3], grads[4], grads[5], grads[6], grads[7...  39.9 us
    all_gather x2, waiting for transfers between devices, carried_in(): gathered = jax.tree.map(lambda a: lax.all_gather(a, axis), part)  30.8 us
  transfers between devices with their start and end apart: 15, of which 13 were waited for; matrix products, arithmetic and copies ran while one was open for 8% of the time, Pallas kernels for 0%

profile of v1, /device:TPU:0, one launch (start us, length us, event | category | flops | bytes accessed | tf_op | source)
XLA Modules:
  0.0 705.1 jit_solution(8547581576306912661)
XLA Ops:
  8.7 2.4 collective-permute-start.1
  12.3 43.7 %all_gather.32 = bf16[768,24]{1,0:T(8,128)(2,1)S(1)} all-gather(bf16[24,24]{1,0:T(8,128)(2,1)} %param.24), channel_id=1, replica_groups=mesh['seq'=8,'span'=4] {'seq','span'}, dimensions={0}, use_global_device_ids=true | all-gather | bytes 38016 | tf_op jit(solution)/shard_map/all_gather | solution.py:174
  61.2 2.0 fusion.122
  63.8 7.9 %all-gather.8.cloned.1.call-done = bf16[768,1792]{1,0:T(8,128)(2,1)} async-done(((bf16[24,1792]{1,0:T(8,128)(2,1)}), bf16[768,1792]{1,0:T(8,128)(2,1)}) %all-gather.8.cloned.1.call-update) | async-done | bytes 2752528 | tf_op jit(solution)/shard_map/all_gather | solution.py:173
  71.7 2.5 convolution_convert_fusion
  74.3 2.1 collective-permute-start
  77.3 1.8 fusion.32
  79.5 1.7 fusion.66
  84.2 6.5 all_gather.33
  91.0 19.8 %all-gather.14.cloned.1.call-done = f32[96,64,128]{2,1,0:T(8,128)} async-done(((f32[24,64,128]{2,1,0:T(8,128)}), f32[96,64,128]{2,1,0:T(8,128)}) %all-gather.14.cloned.1.call-update) | async-done | bytes 3145744 | tf_op jit(solution)/shard_map/all_gather | solution.py:50
  111.8 3.3 fusion.19
  116.3 54.4 %all-gather.10.cloned.1.call-done = bf16[768,1536]{1,0:T(8,128)(2,1)} async-done(((bf16[24,1536]{1,0:T(8,128)(2,1)}), bf16[768,1536]{1,0:T(8,128)(2,1)}) %all-gather.10.cloned.1.call-update) | async-done | bytes 2359312 | tf_op jit(solution)/shard_map/all_gather | solution.py:172
  170.8 3.3 multiply_reduce_fusion.11
  174.1 55.2 %all-gather.12.cloned.1.call-done = bf16[1536,768]{1,0:T(8,128)(2,1)} async-done(((bf16[48,768]{1,0:T(8,128)(2,1)}), bf16[1536,768]{1,0:T(8,128)(2,1)}) %all-gather.12.cloned.1.call-update) | async-done | bytes 2359312 | tf_op jit(solution)/shard_map/all_gather | solution.py:218
  229.3 3.5 multiply_reduce_fusion.7
  232.8 2.2 fusion.44
  235.0 2.3 copy.119
  237.3 2.8 fusion.50
  241.3 2.3 copy.117
  243.5 2.4 mul.732
  246.0 2.4 copy.118
  248.4 5.6 fusion.40
  256.6 11.0 %all-gather.16.cloned.1.call-done = f32[96,64,128]{2,1,0:T(8,128)} async-done(((f32[24,64,128]{2,1,0:T(8,128)}), f32[96,64,128]{2,1,0:T(8,128)}) %all-gather.16.cloned.1.call-update) | async-done | bytes 3145744 | tf_op jit(solution)/shard_map/all_gather | solution.py:50
  267.6 6.2 while.28
  274.7 2.3 multiply_reduce_fusion.6
  278.5 2.8 fusion.13
  281.4 2.4 copy.122
  283.9 2.8 fusion.137
  290.6 2.0 fusion.142
  293.9 1.5 bitcast_add_fusion.2
  296.9 2.6 reduce_window_sum.30
  299.4 1.5 copy.126
  302.2 1.9 slice_bitcast_fusion
  304.1 2.1 fusion.139
  310.5 6.8 fusion.33
  320.4 3.1 fusion.80
  323.5 4.2 collective-permute-done.3
  327.8 1.5 collective-permute-start.4
  329.4 11.8 %collective-permute-done.4 = bf16[4,48,768]{2,1,0:T(8,128)(2,1)S(1)} collective-permute-done((bf16[4,48,768]{2,1,0:T(8,128)(2,1)S(1)}, bf16[4,48,768]{2,1,0:T(8,128)(2,1)S(1)}, u32[]{:S(2)}, u32[]{:S(2)}) %collective-permute-start.4) | collective-permute-done | bytes 294944 | tf_op jit(solution)/shard_map/ppermute | solution.py:29
  341.4 1.6 collective-permute-start.5
  342.9 25.9 %collective-permute-done.5 = bf16[8,48,768]{2,1,0:T(8,128)(2,1)S(1)} collective-permute-done((bf16[8,48,768]{2,1,0:T(8,128)(2,1)S(1)}, bf16[8,48,768]{2,1,0:T(8,128)(2,1)S(1)}, u32[]{:S(2)}, u32[]{:S(2)}) %collective-permute-start.5) | collective-permute-done | bytes 589856 | tf_op jit(solution)/shard_map/ppermute | solution.py:29
  369.2 3.3 collective-permute-start.6
  372.5 67.9 %collective-permute-done.6 = bf16[16,48,768]{2,1,0:T(8,128)(2,1)S(1)} collective-permute-done((bf16[16,48,768]{2,1,0:T(8,128)(2,1)S(1)}, bf16[16,48,768]{2,1,0:T(8,128)(2,1)S(1)}, u32[]{:S(2)}, u32[]{:S(2)}) %collective-permute-start.6) | collective-permute-done | bytes 1179680 | tf_op jit(solution)/shard_map/ppermute | solution.py:29
  449.1 39.9 %all-reduce.15 = (f32[768]{0:T(1024)}, f32[4,1792]{1,0:T(4,128)}, f32[1792]{0:T(1024)}, f32[24]{0:T(128)}, f32[24]{0:T(128)}, /*index=5*/f32[24]{0:T(128)}, f32[1536]{0:T(1024)}) all-reduce(f32[768]{0:T(1024)S(1)} %get-tuple-element.219, f32[4,1792]{1,0:T(4,128)S(1)} %pad_add_fusion.2, ...), channel_id=1, replica_groups=mesh['seq'=8,'span'=4] {'seq','span'}, use_global_device_ids=true, to_apply=%region_18.19 | all-reduce | flops 11336 | bytes 90688 | tf_op jit(solution)/shard_map/psum | solution.py:287
  490.0 95.6 %all-reduce.18.cloned.1.call-done = f32[768,3352]{1,0:T(8,128)} async-done(((f32[768,3352]{1,0:T(8,128)}), f32[768,3352]{1,0:T(8,128)}) %all-reduce.18.cloned.1.call-update) | async-done | bytes 10297360
  586.9 1.7 dynamic-slice.10
  588.6 1.6 constant_dynamic-slice_fusion
  590.2 108.0 %reduce-scatter.2.cloned.1.call-done = f32[48,768]{1,0:T(8,128)} async-done(((f32[1536,768]{1,0:T(8,128)}), f32[48,768]{1,0:T(8,128)}) %reduce-scatter.2.cloned.1.call-update) | async-done | bytes 147472 | tf_op jit(solution)/shard_map/reduce_scatter | solution.py:268
  (285 shorter events, 53.5 us)
Async XLA Ops:
  7.2 64.6 %all-gather.8.cloned.1.call-start = ((), (), s32[]{:S(2)}) async-start(), calls=%async_computation.1 | async-start | bytes 2838528 | tf_op jit(solution)/shard_map/all_gather | solution.py:173
  7.9 102.9 %all-gather.14.cloned.1.call-start = ((), (), s32[]{:S(2)}) async-start(), calls=%async_computation.5 | async-start | bytes 3932160 | tf_op jit(solution)/shard_map/all_gather | solution.py:50
  8.7 51.8 %collective-permute-start.1 = (bf16[1,3]{1,0:T(2,128)(2,1)S(1)}, bf16[1,3]{1,0:T(2,128)(2,1)S(1)}, u32[]{:S(2)}, u32[]{:S(2)}) collective-permute-start(bf16[1,3]{1,0:T(2,128)(2,1)S(1)} %add_convert_fusion.1), channel_id=1, source_target_pairs={{0,1},{1,2},{2,3},{4,5},{5,6},{6,7},{8,9},{9,10},{10,11},{12,13},{... | collective-permute-start | bytes 26 | tf_op jit(solution)/shard_map/ppermute | solution.py:43
  57.1 17.1 %copy-start.85 = (f32[128]{0:T(128)}, f32[128]{0:T(128)S(1)}, u32[]{:S(2)}) copy-start(f32[128]{0:T(128)S(1)} %fusion.74) | copy-start | bytes 1540
  57.8 16.4 %copy-start.82 = (f32[24]{0:T(128)}, f32[24]{0:T(128)S(1)}, u32[]{:S(2)}) copy-start(f32[24]{0:T(128)S(1)} %exponential_negate_fusion) | copy-start | bytes 292
  57.8 112.9 %copy-start.54 = (f32[128]{0:T(128)}, f32[128]{0:T(128)S(1)}, u32[]{:S(2)}) copy-start(f32[128]{0:T(128)S(1)} %fusion.125) | copy-start | bytes 1540
  59.0 15.2 %copy-start.23 = (f32[128,24]{0,1:T(8,128)}, f32[128,24]{0,1:T(8,128)S(1)}, u32[]{:S(2)}) copy-start(f32[128,24]{0,1:T(8,128)S(1)} %convolution_add_fusion.3) | copy-start | bytes 36868
  60.5 16.8 %copy-start.34 = (f32[1792]{0:T(1024)}, f32[1792]{0:T(1024)S(1)}, u32[]{:S(2)}) copy-start(f32[1792]{0:T(1024)S(1)} %get-tuple-element.221) | copy-start | bytes 21508
  60.5 16.8 %copy-start.36 = (f32[1792]{0:T(1024)}, f32[1792]{0:T(1024)S(1)}, u32[]{:S(2)}) copy-start(f32[1792]{0:T(1024)S(1)} %get-tuple-element.222) | copy-start | bytes 21508
  60.5 16.8 %copy-start.38 = (f32[1792]{0:T(1024)}, f32[1792]{0:T(1024)S(1)}, u32[]{:S(2)}) copy-start(f32[1792]{0:T(1024)S(1)} %get-tuple-element.223) | copy-start | bytes 21508
  60.5 16.8 %copy-start.40 = (f32[1792]{0:T(1024)}, f32[1792]{0:T(1024)S(1)}, u32[]{:S(2)}) copy-start(f32[1792]{0:T(1024)S(1)} %get-tuple-element.224) | copy-start | bytes 21508
  61.2 18.0 %copy-start.65 = (f32[128]{0:T(128)}, f32[128]{0:T(128)S(1)}, u32[]{:S(2)}) copy-start(f32[128]{0:T(128)S(1)} %get-tuple-element.273) | copy-start | bytes 1540
  61.2 18.0 %copy-start.68 = (f32[128]{0:T(128)}, f32[128]{0:T(128)S(1)}, u32[]{:S(2)}) copy-start(f32[128]{0:T(128)S(1)} %get-tuple-element.274) | copy-start | bytes 1540
  61.2 18.0 %copy-start.71 = (f32[128]{0:T(128)}, f32[128]{0:T(128)S(1)}, u32[]{:S(2)}) copy-start(f32[128]{0:T(128)S(1)} %get-tuple-element.275) | copy-start | bytes 1540
  63.2 14.1 %copy-start.74 = (f32[128]{0:T(128)}, f32[128]{0:T(128)S(1)}, u32[]{:S(2)}) copy-start(f32[128]{0:T(128)S(1)} %get-tuple-element.279) | copy-start | bytes 1540
  63.2 19.6 %copy-start.80 = (f32[128]{0:T(128)}, f32[128]{0:T(128)S(1)}, u32[]{:S(2)}) copy-start(f32[128]{0:T(128)S(1)} %get-tuple-element.280) | copy-start | bytes 1540
  63.8 15.7 %copy-start.31 = (f32[128,24]{0,1:T(8,128)}, f32[128,24]{0,1:T(8,128)S(1)}, u32[]{:S(2)}) copy-start(f32[128,24]{0,1:T(8,128)S(1)} %get-tuple-element.271) | copy-start | bytes 36868
  63.8 48.0 %copy-start.60 = (f32[24,128]{1,0:T(8,128)}, f32[24,128]{1,0:T(8,128)S(1)}, u32[]{:S(2)}) copy-start(f32[24,128]{1,0:T(8,128)S(1)} %get-tuple-element.272) | copy-start | bytes 36868
  63.8 13.5 %copy-start.63 = (f32[1792]{0:T(1024)S(1)}, f32[1792]{0:T(1024)}, u32[]{:S(2)}) copy-start(f32[1792]{0:T(1024)} %param.26) | copy-start | bytes 21508
  74.3 4.9 copy-start.5
  74.3 3.0 collective-permute-start
  79.1 175.1 %copy-start.2 = (f32[1,128,1792]{2,1,0:T(8,128)}, f32[1,128,1792]{2,1,0:T(8,128)S(1)}, u32[]{:S(2)}) copy-start(f32[1,128,1792]{2,1,0:T(8,128)S(1)} %get-tuple-element.261) | copy-start | bytes 2752516
  81.2 89.5 %all-gather.10.cloned.1.call-start = ((), (), s32[]{:S(2)}) async-start(), calls=%async_computation.2 | async-start | bytes 2433024 | tf_op jit(solution)/shard_map/all_gather | solution.py:172
  82.0 147.3 %all-gather.12.cloned.1.call-start = ((), (), s32[]{:S(2)}) async-start(), calls=%async_computation.3 | async-start | bytes 2433024 | tf_op jit(solution)/shard_map/all_gather | solution.py:218
  82.5 185.0 %all-gather.16.cloned.1.call-start = ((), (), s32[]{:S(2)}) async-start(), calls=%async_computation.6 | async-start | bytes 3932160 | tf_op jit(solution)/shard_map/all_gather | solution.py:50
  82.7 29.1 %copy-start.57 = (f32[24,128]{1,0:T(8,128)}, f32[24,128]{1,0:T(8,128)S(1)}, u32[]{:S(2)}) copy-start(f32[24,128]{1,0:T(8,128)S(1)} %copy.108) | copy-start | bytes 36868
  82.8 165.5 %copy-start.52 = (pred[128,128]{1,0:T(8,128)(4,1)}, pred[128,128]{1,0:T(8,128)(4,1)S(1)}, u32[]{:S(2)}) copy-start(pred[128,128]{1,0:T(8,128)(4,1)S(1)} %fusion.96) | copy-start | bytes 49156
  91.0 20.8 %copy-start.42 = (f32[128,128]{1,0:T(8,128)}, f32[128,128]{1,0:T(8,128)S(1)}, u32[]{:S(2)}) copy-start(f32[128,128]{1,0:T(8,128)S(1)} %fusion.92) | copy-start | bytes 196612
  110.9 4.2 copy-start.84
  115.1 55.6 %copy-start.9 = (bf16[1,128,768]{2,1,0:T(8,128)(2,1)S(1)}, bf16[1,128,768]{2,1,0:T(8,128)(2,1)}, u32[]{:S(2)}) copy-start(bf16[1,128,768]{2,1,0:T(8,128)(2,1)} %param.20) | copy-start | bytes 589828
  115.1 55.6 %copy-start.28 = (f32[768]{0:T(1024)S(1)}, f32[768]{0:T(1024)}, u32[]{:S(2)}) copy-start(f32[768]{0:T(1024)} %param.21) | copy-start | bytes 9220
  116.3 113.0 %copy-start.29 = (f32[1536]{0:T(1024)S(1)}, f32[1536]{0:T(1024)}, u32[]{:S(2)}) copy-start(f32[1536]{0:T(1024)} %param.30) | copy-start | bytes 18436
  174.1 58.7 %copy-start.77 = (f32[128]{0:T(128)}, f32[128]{0:T(128)S(1)}, u32[]{:S(2)}) copy-start(f32[128]{0:T(128)S(1)} %fusion.126) | copy-start | bytes 1540
  240.1 345.5 %all-reduce.18.cloned.1.call-start = ((), (), s32[]{:S(2)}) async-start(), calls=%async_computation.7 | async-start | bytes 21233664
  243.5 4.8 copy-start.43
  243.5 4.8 copy-start.58
  243.5 4.8 copy-start.61
  248.4 6.1 copy-start.7
  248.4 6.1 copy-start.15
  278.5 5.3 copy-start.12
  300.9 6.7 collective-permute-start.7
  317.3 380.9 %reduce-scatter.2.cloned.1.call-start = ((), (), s32[]{:S(2)}) async-start(), calls=%async_computation.4 | async-start | bytes 4866048 | tf_op jit(solution)/shard_map/reduce_scatter | solution.py:268
  318.2 2.0 collective-permute-start.2
  320.3 7.5 %collective-permute-start.3 = (bf16[2,48,768]{2,1,0:T(8,128)(2,1)S(1)}, bf16[2,48,768]{2,1,0:T(8,128)(2,1)S(1)}, u32[]{:S(2)}, u32[]{:S(2)}) collective-permute-start(bf16[2,48,768]{2,1,0:T(8,128)(2,1)S(1)} %get-tuple-element.269), channel_id=1, source_target_pairs={{0,2},{1,3},{2,0},{3,1},{4,6},{5,7},{6,4},{7,5},{8,10},{9,11},{10,... | collective-permute-start | bytes 442376 | tf_op jit(solution)/shard_map/ppermute | solution.py:29
  327.8 13.4 %collective-permute-start.4 = (bf16[4,48,768]{2,1,0:T(8,128)(2,1)S(1)}, bf16[4,48,768]{2,1,0:T(8,128)(2,1)S(1)}, u32[]{:S(2)}, u32[]{:S(2)}) collective-permute-start(bf16[4,48,768]{2,1,0:T(8,128)(2,1)S(1)} %bitcast.299), channel_id=1, source_target_pairs={{0,4},{1,5},{2,6},{3,7},{4,0},{5,1},{6,2},{7,3},{8,12},{9,13},{10,... | collective-permute-start | bytes 884744 | tf_op jit(solution)/shard_map/ppermute | solution.py:29
  341.4 27.5 %collective-permute-start.5 = (bf16[8,48,768]{2,1,0:T(8,128)(2,1)S(1)}, bf16[8,48,768]{2,1,0:T(8,128)(2,1)S(1)}, u32[]{:S(2)}, u32[]{:S(2)}) collective-permute-start(bf16[8,48,768]{2,1,0:T(8,128)(2,1)S(1)} %bitcast.297), channel_id=1, source_target_pairs={{0,8},{1,9},{2,10},{3,11},{4,12},{5,13},{6,14},{7,15},{8,0},{9,1},... | collective-permute-start | bytes 1769480 | tf_op jit(solution)/shard_map/ppermute | solution.py:29
  369.2 71.2 %collective-permute-start.6 = (bf16[16,48,768]{2,1,0:T(8,128)(2,1)S(1)}, bf16[16,48,768]{2,1,0:T(8,128)(2,1)S(1)}, u32[]{:S(2)}, u32[]{:S(2)}) collective-permute-start(bf16[16,48,768]{2,1,0:T(8,128)(2,1)S(1)} %bitcast.293), channel_id=1, source_target_pairs={{0,16},{1,17},{2,18},{3,19},{4,20},{5,21},{6,22},{7,23},{8,24},{9,... | collective-permute-start | bytes 3538952 | tf_op jit(solution)/shard_map/ppermute | solution.py:29
  447.7 41.4 %copy-start.86 = (f32[128]{0:T(128)S(1)}, f32[128]{0:T(128)}, u32[]{:S(2)}) copy-start(f32[128]{0:T(128)} %copy-done.85) | copy-start | bytes 1540
  (57 other events, 138.2 us)
Sparse Core Ops, SparseCore 0:
  10.9 60.8 all-gather.7
  81.3 29.4 all-gather.13
  113.7 56.9 all-gather.9
  173.5 55.7 all-gather.11
  240.2 27.2 all-gather.15
  317.4 268.0 all-reduce.17
  591.6 106.5 reduce-scatter.1
